TPU v7x, 32 devices: a whole 2x2x4 slice. The times are simulated.
32 devices in a mesh: cen: 8 (over y, x, core), grp: 4 (over z).
Axes of the slice: x: 2, y: 2, z: 4, core: 2. Of those that a mesh axis runs over, the one named last changes fastest.
Arguments:
- centers: bfloat16 [65536, 1024], P(('cen', 'grp')), may hold values from -2 to 2
- coefficients: float32 [65536, 256], P(('cen', 'grp')), may hold values from -0.09375 to 0.09375
- batch_index: int32 [256], P(('cen', 'grp')), may hold values from 0 to 65535, as said below
- batch_labels: float32 [256, 256], P(('cen', 'grp')), may hold values from -24 to 24
- nystrom_index: int32 [16384], P(('cen', 'grp')), may hold values from 0 to 65535, as said below
- eigenvectors: float32 [16384, 512], P(('cen', 'grp')), may hold values from -0.046875 to 0.046875
- eigen_weights: float32 [512], replicated, may hold values from 0.002 to 0.05
Outputs:
- residual: float32 [256, 256], P(('cen', 'grp'))
- correction: float32 [16384, 256], P(('cen', 'grp'))
Inputs may be any that keep to these rules, and one draw needn't show every extreme that they name: `batch_index`: for each j, entries 8 * j to 8 * j + 7 are distinct rows among j * 2048 to j * 2048 + 2047. `nystrom_index`: for each j, entries 512 * j to 512 * j + 511 are distinct rows among j * 2048 to j * 2048 + 2047.
All inputs are finite; a program needn't handle non-finite values.
Results may differ from a plain program's by a relative error of at most 0.0003.
Values may be sent and summed in bfloat16 or wider, within the bound.
No kernel may reach another device: no remote copies, remote signals or barrier semaphores. Data moves between devices by JAX's collectives and lax.ppermute only.
A program may use at most 64 MiB of HBM per device.

v0:
```python
import jax
import jax.numpy as jnp
from jax import lax
from jax.sharding import PartitionSpec as P


def inner_kernel(left, right):
    scores = lax.dot_general(
        left, right, (((1,), (1,)), ((), ())), preferred_element_type=jnp.float32
    )
    return jnp.exp(scores / 32.0)


def exact_dot(left, right):
    return jnp.dot(left, right, precision=lax.Precision.HIGHEST, preferred_element_type=jnp.float32)


def body(
    centers, coefficients, batch_index, batch_labels, nystrom_index, eigenvectors, eigen_weights
):
    center_count = centers.shape[0]
    owned_rows = jnp.take(centers, batch_index % center_count, axis=0)
    batch_x = lax.all_gather(owned_rows, ("cen", "grp"), axis=0, tiled=True)
    partial_pred = exact_dot(inner_kernel(batch_x, centers), coefficients)
    nystrom_x = jnp.take(centers, nystrom_index % center_count, axis=0)
    nystrom_kernel = inner_kernel(nystrom_x, batch_x)
    batch_rows = batch_labels.shape[0]
    first_row = lax.axis_index(("cen", "grp")) * batch_rows
    own_part = lax.dynamic_slice_in_dim(partial_pred, first_row, batch_rows, 0) - batch_labels
    summand = lax.dynamic_update_slice_in_dim(partial_pred, own_part, first_row, 0)
    residual_all = lax.psum(summand, ("cen", "grp"))
    own_residual = lax.dynamic_slice_in_dim(residual_all, first_row, batch_rows, 0)
    local_products = exact_dot(nystrom_kernel, residual_all)
    projected = lax.psum(exact_dot(eigenvectors.T, local_products), ("cen", "grp"))
    correction = exact_dot(eigenvectors, eigen_weights[:, None] * projected)
    return (own_residual, correction)


def solution(mesh):
    in_specs = (
        P(("cen", "grp"), None),
        P(("cen", "grp"), None),
        P(("cen", "grp")),
        P(("cen", "grp"), None),
        P(("cen", "grp")),
        P(("cen", "grp"), None),
        P(),
    )
    out_specs = (P(("cen", "grp"), None), P(("cen", "grp"), None))
    return jax.shard_map(body, mesh=mesh, in_specs=in_specs, out_specs=out_specs, check_vma=False)
```

profile of v0, /device:TPU:0, one launch (start us, length us, event | category | flops | bytes accessed | tf_op | source)
XLA Modules:
  0.0 365.1 jit_solution(11219667917849283521)
XLA Ops:
  7.2 0.0 copy-start
  7.2 0.0 all-reduce.3.cloned.1.call-start
  7.2 0.8 compare_and_fusion.1
  8.0 3.3 gather_fusion
  11.4 0.1 broadcast_select_fusion
  11.4 73.9 %all_gather.3 = bf16[256,1024]{1,0:T(8,128)(2,1)S(1)} all-gather(bf16[8,1024]{1,0:T(8,128)(2,1)S(1)} %broadcast_select_fusion), channel_id=1, replica_groups=mesh['cen'=8,'grp'=4] {'cen','grp'}, dimensions={0}, use_global_device_ids=true | all-gather | bytes 540672 | tf_op jit(solution)/shard_map/all_gather | solution.py:23
  85.4 0.8 copy-done.3
  86.2 4.9 %fusion = f32[256,2048]{1,0:T(8,128)} fusion(bf16[256,1024]{1,0:T(8,128)(2,1)S(1)} %all_gather.3, bf16[2048,1024]{1,0:T(8,128)(2,1)} %param.7), kind=kOutput, calls=%fused_computation.3 | convolution fusion | flops 1074266112 | bytes 6815744 | tf_op jit(solution)/shard_map/dot_general | solution.py:8
  91.1 0.0 copy-done
  91.1 3.5 fusion.10
  94.6 0.0 copy-done.4
  94.6 0.7 copy-done.2
  95.3 0.0 all-reduce.3.cloned.1.call-update
  95.4 0.0 all-reduce.5.cloned.1.call-start
  95.5 6.2 %gather_fusion.1 = bf16[512,1024]{1,0:T(8,128)(2,1)} fusion(bf16[2048,1024]{1,0:T(8,128)(2,1)} %param.7, s32[1024]{0:T(1024)S(1)} %pad_clamp_fusion), kind=kCustom, calls=%fused_computation.1 | custom fusion | bytes 2099200 | tf_op jit(solution)/shard_map/jit(_take)/gather | solution.py:25
  101.7 2.8 fusion.1
  104.4 114.0 %all-reduce.3.cloned.1.call-done = f32[256,256]{1,0:T(8,128)} async-done(((f32[256,256]{1,0:T(8,128)}), f32[256,256]{1,0:T(8,128)}) %all-reduce.3.cloned.1.call-update) | async-done | bytes 262160 | tf_op jit(solution)/shard_map/psum | solution.py:31
  218.5 1.7 fusion.11
  220.2 2.6 convolution_bitcast_fusion.1
  222.8 0.0 all-reduce.5.cloned.1.call-update
  222.8 1.3 constant_dynamic-slice_fusion
  224.1 128.4 %all-reduce.5.cloned.1.call-done = f32[512,256]{1,0:T(8,128)} async-done(((f32[512,256]{1,0:T(8,128)}), f32[512,256]{1,0:T(8,128)}) %all-reduce.5.cloned.1.call-update) | async-done | bytes 524304 | tf_op jit(solution)/shard_map/psum | solution.py:34
  352.5 3.8 %convolution_bitcast_fusion = f32[512,256]{0,1:T(8,128)} fusion(f32[512,512]{1,0:T(8,128)S(1)} %copy-done.1, f32[512,256]{1,0:T(8,128)} %all-reduce.5.cloned.1.call-done, f32[512]{0:T(512)S(1)} %copy-done.5), kind=kOutput, calls=%fused_computation.6 | convolution fusion | flops 805437440 | bytes 2099200 | tf_op jit(solution)/shard_map/dot_general | solution.py:15
  356.2 2.0 copy.9
  (13 shorter events, 0.1 us)
Async XLA Ops:
  7.2 83.9 %copy-start = (f32[2048,256]{1,0:T(8,128)S(1)}, f32[2048,256]{1,0:T(8,128)}, u32[]{:S(2)}) copy-start(f32[2048,256]{1,0:T(8,128)} %param.8) | copy-start | bytes 6291460
  7.2 211.3 %all-reduce.3.cloned.1.call-start = ((), (), s32[]{:S(2)}) async-start(), calls=%async_computation | async-start | bytes 524288 | tf_op jit(solution)/shard_map/psum | solution.py:31
  85.4 0.8 copy-start.3
  91.1 3.5 copy-start.4
  91.1 4.3 %copy-start.6 = (s32[512]{0:T(512)S(1)}, s32[512]{0:T(512)}, u32[]{:S(2)}) copy-start(s32[512]{0:T(512)} %param.11) | copy-start | bytes 6148
  94.6 0.7 copy-start.2
  95.4 257.1 %all-reduce.5.cloned.1.call-start = ((), (), s32[]{:S(2)}) async-start(), calls=%async_computation.1 | async-start | bytes 1048576 | tf_op jit(solution)/shard_map/psum | solution.py:34
  101.7 118.5 %copy-start.1 = (f32[512,512]{1,0:T(8,128)S(1)}, f32[512,512]{1,0:T(8,128)}, u32[]{:S(2)}) copy-start(f32[512,512]{1,0:T(8,128)} %param.12) | copy-start | bytes 3145732
  104.4 248.0 %copy-start.5 = (f32[512]{0:T(512)S(1)}, f32[512]{0:T(512)}, u32[]{:S(2)}) copy-start(f32[512]{0:T(512)} %param.13) | copy-start | bytes 6148
Sparse Core Ops, SparseCore 0:
  95.5 122.9 all-reduce.2
  224.3 128.1 all-reduce.4
where the time goes:
time: 366 us; the launch traced here: 365 us
  waiting for transfers between devices  242 us (66%)
  blocking collectives  73.9 us (20%)
  matrix products  19.3 us (5%)
  local copies, waits for them, and re-layouts  14.4 us (4%)
  between operations  14.1 us (4%)
    psum x1, waiting for transfers between devices, body(): lax.psum(exact_dot(eigenvectors.T, local_products), ('cen', 'grp'))  128 us
    psum x1, waiting for transfers between devices, body(): residual_all = lax.psum(summand, ('cen', 'grp'))  114 us
    all_gather x1, blocking collectives, body(): batch_x = lax.all_gather(owned_rows, ('cen', 'grp'), axis=0, tiled=True)  73.9 us
    dot_general x4, matrix products, exact_dot(): jnp.dot(left, right, precision=lax.Precision.HIGHEST, preferred_element_t...  11.6 us
    dot_general x2, matrix products, inner_kernel(): lax.dot_general(left, right, (((1,), (1,)), ((), ())), preferred_element_...  7.7 us
  transfers between devices with their start and end apart: 2, of which 2 were waited for; matrix products, arithmetic and copies ran while one was open for 3% of the time, Pallas kernels for 0%

commit v1 on v0

--- a/solution.py
+++ b/solution.py
@@ -31,7 +31,9 @@
     residual_all = lax.psum(summand, ("cen", "grp"))
     own_residual = lax.dynamic_slice_in_dim(residual_all, first_row, batch_rows, 0)
     local_products = exact_dot(nystrom_kernel, residual_all)
-    projected = lax.psum(exact_dot(eigenvectors.T, local_products), ("cen", "grp"))
+    projected = exact_dot(eigenvectors.T, local_products)
+    for axis in ("grp", "cen"):
+        projected = lax.psum(projected, axis)
     correction = exact_dot(eigenvectors, eigen_weights[:, None] * projected)
     return (own_residual, correction)
 

time: 366 us -> 331 us (0.904)
  waiting for transfers between devices: 242 us -> 208 us
    psum x1 -> x2, waiting for transfers between devices: 128 us -> 94.1 us  [body(): projected = lax.psum(projected, axis)]
  transfers between devices with their start and end apart: 2 -> 3, of which waited for: 2 -> 3; matrix products, arithmetic and copies ran while one was open for 3% -> 3% of each run, Pallas kernels for 0% -> 0%
where the time goes in v1:
time: 331 us
  waiting for transfers between devices  208 us (63%)
  blocking collectives  73.9 us (22%)
  matrix products  19.3 us (6%)
  local copies, waits for them, and re-layouts  14.4 us (4%)
  between operations  13.8 us (4%)
    psum x1, waiting for transfers between devices, body(): residual_all = lax.psum(summand, ('cen', 'grp'))  114 us
    psum x2, waiting for transfers between devices, body(): projected = lax.psum(projected, axis)  94.1 us
    all_gather x1, blocking collectives, body(): batch_x = lax.all_gather(owned_rows, ('cen', 'grp'), axis=0, tiled=True)  73.9 us
    dot_general x4, matrix products, exact_dot(): jnp.dot(left, right, precision=lax.Precision.HIGHEST, preferred_element_t...  11.6 us
    dot_general x2, matrix products, inner_kernel(): lax.dot_general(left, right, (((1,), (1,)), ((), ())), preferred_element_...  7.7 us
  transfers between devices with their start and end apart: 3, of which 3 were waited for; matrix products, arithmetic and copies ran while one was open for 3% of the time, Pallas kernels for 0%

profile of v1, /device:TPU:0, one launch (start us, length us, event | category | flops | bytes accessed | tf_op | source)
XLA Modules:
  0.0 330.6 jit_solution(1303284142650349051)
XLA Ops:
  7.2 0.0 all-reduce.4.cloned.1.call-start
  7.2 0.8 compare_and_fusion.1
  8.0 3.3 %gather_fusion = bf16[8,1024]{1,0:T(8,128)(2,1)S(1)} fusion(bf16[2048,1024]{1,0:T(8,128)(2,1)} %param.7, s32[1024]{0:T(1024)S(1)} %pad_clamp_fusion.1), kind=kCustom, calls=%fused_computation | custom fusion | bytes 32800 | tf_op jit(solution)/shard_map/jit(_take)/gather | solution.py:22
  11.4 0.1 broadcast_select_fusion
  11.4 73.9 %all_gather.3 = bf16[256,1024]{1,0:T(8,128)(2,1)S(1)} all-gather(bf16[8,1024]{1,0:T(8,128)(2,1)S(1)} %broadcast_select_fusion), channel_id=1, replica_groups=mesh['cen'=8,'grp'=4] {'cen','grp'}, dimensions={0}, use_global_device_ids=true | all-gather | bytes 540672 | tf_op jit(solution)/shard_map/all_gather | solution.py:23
  85.4 0.8 copy-done.3
  86.2 4.9 %fusion = f32[256,2048]{1,0:T(8,128)} fusion(bf16[256,1024]{1,0:T(8,128)(2,1)S(1)} %all_gather.3, bf16[2048,1024]{1,0:T(8,128)(2,1)} %param.7), kind=kOutput, calls=%fused_computation.3 | convolution fusion | flops 1074266112 | bytes 6815744 | tf_op jit(solution)/shard_map/dot_general | solution.py:8
  91.1 3.5 %fusion.10 = f32[256,256]{1,0:T(8,128)S(1)} fusion(f32[256,2048]{1,0:T(8,128)} %fusion, f32[2048,256]{1,0:T(8,128)S(1)} %copy-done), kind=kOutput, calls=%fused_computation.31 | convolution fusion | flops 1610612736 | bytes 4456448 | tf_op jit(solution)/shard_map/dot_general | solution.py:15
  94.6 0.7 copy-done.2
  95.3 0.0 all-reduce.4.cloned.1.call-update
  95.4 0.0 all-reduce.6.cloned.1.call-start
  95.5 6.2 %gather_fusion.1 = bf16[512,1024]{1,0:T(8,128)(2,1)} fusion(bf16[2048,1024]{1,0:T(8,128)(2,1)} %param.7, s32[1024]{0:T(1024)S(1)} %pad_clamp_fusion), kind=kCustom, calls=%fused_computation.1 | custom fusion | bytes 2099200 | tf_op jit(solution)/shard_map/jit(_take)/gather | solution.py:25
  101.7 2.8 fusion.1
  104.4 114.0 %all-reduce.4.cloned.1.call-done = f32[256,256]{1,0:T(8,128)} async-done(((f32[256,256]{1,0:T(8,128)}), f32[256,256]{1,0:T(8,128)}) %all-reduce.4.cloned.1.call-update) | async-done | bytes 262160 | tf_op jit(solution)/shard_map/psum | solution.py:31
  218.5 1.7 fusion.11
  220.2 2.6 convolution_bitcast_fusion.1
  222.8 0.0 all-reduce.6.cloned.1.call-update
  222.8 0.0 all-reduce.8.cloned.1.call-start
  222.9 37.7 %all-reduce.6.cloned.1.call-done = f32[512,256]{1,0:T(8,128)} async-done(((f32[512,256]{1,0:T(8,128)}), f32[512,256]{1,0:T(8,128)}) %all-reduce.6.cloned.1.call-update) | async-done | bytes 524304 | tf_op jit(solution)/shard_map/psum | solution.py:36
  260.5 0.0 all-reduce.8.cloned.1.call-update
  260.5 1.3 constant_dynamic-slice_fusion
  261.9 56.4 %all-reduce.8.cloned.1.call-done = f32[512,256]{1,0:T(8,128)} async-done(((f32[512,256]{1,0:T(8,128)}), f32[512,256]{1,0:T(8,128)}) %all-reduce.8.cloned.1.call-update) | async-done | bytes 524304 | tf_op jit(solution)/shard_map/psum | solution.py:36
  318.3 3.8 %convolution_bitcast_fusion = f32[512,256]{0,1:T(8,128)} fusion(f32[512,512]{1,0:T(8,128)S(1)} %copy-done.1, f32[512,256]{1,0:T(8,128)} %all-reduce.8.cloned.1.call-done, f32[512]{0:T(512)S(1)} %copy-done.5), kind=kOutput, calls=%fused_computation.6 | convolution fusion | flops 805437440 | bytes 2099200 | tf_op jit(solution)/shard_map/dot_general | solution.py:15
  322.1 2.0 copy.9
  (16 shorter events, 0.1 us)
Async XLA Ops:
  7.2 83.9 %copy-start = (f32[2048,256]{1,0:T(8,128)S(1)}, f32[2048,256]{1,0:T(8,128)}, u32[]{:S(2)}) copy-start(f32[2048,256]{1,0:T(8,128)} %param.8) | copy-start | bytes 6291460
  7.2 211.3 %all-reduce.4.cloned.1.call-start = ((), (), s32[]{:S(2)}) async-start(), calls=%async_computation | async-start | bytes 524288 | tf_op jit(solution)/shard_map/psum | solution.py:31
  85.4 0.8 copy-start.3
  91.1 3.5 %copy-start.4 = (f32[8,256]{1,0:T(8,128)S(1)}, f32[8,256]{1,0:T(8,128)}, u32[]{:S(2)}) copy-start(f32[8,256]{1,0:T(8,128)} %param.10) | copy-start | bytes 24580
  91.1 4.3 %copy-start.6 = (s32[512]{0:T(512)S(1)}, s32[512]{0:T(512)}, u32[]{:S(2)}) copy-start(s32[512]{0:T(512)} %param.11) | copy-start | bytes 6148
  94.6 0.7 copy-start.2
  95.4 165.2 %all-reduce.6.cloned.1.call-start = ((), (), s32[]{:S(2)}) async-start(), calls=%async_computation.1 | async-start | bytes 1048576 | tf_op jit(solution)/shard_map/psum | solution.py:36
  101.7 118.5 %copy-start.1 = (f32[512,512]{1,0:T(8,128)S(1)}, f32[512,512]{1,0:T(8,128)}, u32[]{:S(2)}) copy-start(f32[512,512]{1,0:T(8,128)} %param.12) | copy-start | bytes 3145732
  104.4 213.9 %copy-start.5 = (f32[512]{0:T(512)S(1)}, f32[512]{0:T(512)}, u32[]{:S(2)}) copy-start(f32[512]{0:T(512)} %param.13) | copy-start | bytes 6148
  222.8 95.5 %all-reduce.8.cloned.1.call-start = ((), (), s32[]{:S(2)}) async-start(), calls=%async_computation.2 | async-start | bytes 1048576 | tf_op jit(solution)/shard_map/psum | solution.py:36
Sparse Core Ops, SparseCore 0:
  95.5 122.9 all-reduce.3
  222.9 37.5 all-reduce.5
  263.6 54.6 all-reduce.7
